TPU v7x, 256 devices: a whole 4x4x8 slice. The times are simulated.
256 devices in a mesh: rows: 32 (over y, z), tensor: 8 (over x, core).
Axes of the slice: x: 4, y: 4, z: 8, core: 2. Of those that a mesh axis runs over, the one named last changes fastest.
Arguments:
- token_ids: int32 [256, 4], replicated, may hold values from 0 to 65535
- cache_lengths: int32 [256], P('rows'), may hold values from 160 to 1280, as said below
- doc_ids: int32 [256], replicated, may hold values from 0 to 31
- embed_table: bfloat16 [65536, 8192], P('tensor', 'rows'), may hold values from -10.5 to 10.5
- cache_keys: bfloat16 [256, 1280, 1024], P('rows', None, 'tensor'), may hold values from -700 to 700
- cache_values: bfloat16 [256, 1280, 1024], P('rows', None, 'tensor'), may hold values from -6 to 6
- decode_gain: float32 [8192], P('rows'), may hold values from 0.1 to 1.9
- decode_query: bfloat16 [8192, 8192], P('rows', 'tensor'), may hold values from -0.0625 to 0.0625
- decode_key: bfloat16 [8192, 1024], P('rows', 'tensor'), may hold values from -0.0625 to 0.0625
- decode_value: bfloat16 [8192, 1024], P('rows', 'tensor'), may hold values from -0.0625 to 0.0625
- decode_out: bfloat16 [8192, 8192], P('tensor', 'rows'), may hold values from -0.0625 to 0.0625
- reduce_gain: float32 [8192], P('rows'), may hold values from 0.8 to 10
- reduce_query: bfloat16 [8192, 8192], P('rows', 'tensor'), may hold values from -0.0625 to 0.0625
- reduce_key: bfloat16 [8192, 1024], P('rows', 'tensor'), may hold values from -0.0625 to 0.0625
- reduce_value: bfloat16 [8192, 1024], P('rows', 'tensor'), may hold values from -0.0625 to 0.0625
- reduce_out: bfloat16 [8192, 8192], P('tensor', 'rows'), may hold values from -0.0625 to 0.0625
Outputs:
- reduced: bfloat16 [1024, 8192], P(None, 'rows')
Inputs may be any that keep to these rules, and one draw needn't show every extreme that they name: Passage row c holds cache entries at positions below cache_lengths[c]; one row in every draw has a full cache of 1280.
All inputs are finite; a program needn't handle non-finite values.
Results may differ from a plain program's by a relative error of at most 0.035.
The roundings to bfloat16 on the way count: a program that leaves them out, or rounds other values in their place, can miss the bound.
Values may be sent and summed in bfloat16 or wider, within the bound.
A program may use at most 64 MiB of HBM per device.

v0:
```python
import jax
import jax.numpy as jnp
from jax import lax
from jax.sharding import PartitionSpec as P

D = 8192
HEAD_DIM = 128
EPSILON = 1e-05
ROPE_BASE = 500000.0


def rotate(vectors, positions):
    half_dim = vectors.shape[-1] // 2
    frequencies = ROPE_BASE ** (-2.0 * jnp.arange(half_dim, dtype=jnp.float32) / vectors.shape[-1])
    angles = positions.astype(jnp.float32)[..., None] * frequencies
    cosine = jnp.cos(angles)
    sine_part = jnp.sin(angles)
    lower_half = vectors[..., :half_dim]
    upper_half = vectors[..., half_dim:]
    return jnp.concatenate(
        [
            lower_half * cosine - upper_half * sine_part,
            upper_half * cosine + lower_half * sine_part,
        ],
        axis=-1,
    )


def width_total(partial_value):
    return lax.psum(partial_value, "tensor")


def row_scale(summed):
    return lax.rsqrt(summed / D + EPSILON)


def head_terms(normed, matrices, squares, groups):
    partial = jnp.concatenate(
        [jnp.dot(normed, matrix, preferred_element_type=jnp.float32) for matrix in matrices], axis=1
    )
    tokens, cols = partial.shape
    own = tokens // groups
    payload = jnp.concatenate(
        [partial.reshape(groups, own * cols), squares.reshape(groups, own)], axis=1
    ).reshape(groups, 8, (own * cols + own) // 8)
    summed = lax.psum_scatter(payload, "rows", scatter_dimension=0, tiled=True)
    summed = summed.reshape(own * cols + own)
    return (summed[: own * cols].reshape(own, cols), summed[own * cols :])


def head_mix(attended, matrix):
    return jnp.dot(
        lax.all_gather(attended, "rows", axis=0, tiled=True),
        matrix,
        preferred_element_type=jnp.float32,
    )


def per_device(
    token_ids,
    cache_lengths,
    doc_ids,
    embed_table,
    cache_keys,
    cache_values,
    decode_gain,
    decode_query,
    decode_key,
    decode_value,
    decode_out,
    reduce_gain,
    reduce_query,
    reduce_key,
    reduce_value,
    reduce_out,
):
    step_count = token_ids.shape[1]
    passage_count = token_ids.shape[0]
    token_count = passage_count * step_count
    own_passages = cache_lengths.shape[0]
    own_tokens = own_passages * step_count
    row_first = lax.axis_index("rows") * own_tokens
    query_cols = decode_query.shape[1]
    kv_cols = decode_key.shape[1]
    local_heads = query_cols // HEAD_DIM
    local_kv = kv_cols // HEAD_DIM
    group_size = local_heads // local_kv
    score_scale = HEAD_DIM ** (-0.5)
    step_ids = jnp.arange(step_count, dtype=jnp.int32)
    vocab_part = embed_table.shape[0]
    local_ids = token_ids.reshape(token_count) - lax.axis_index("tensor") * vocab_part
    inside = (local_ids >= 0) & (local_ids < vocab_part)
    picked = jnp.take(embed_table, jnp.clip(local_ids, 0, vocab_part - 1), axis=0)
    picked = jnp.where(inside[:, None], picked, jnp.zeros_like(picked))
    embedded = width_total(picked).astype(jnp.float32)
    row_groups = token_count // own_tokens
    normed = (embedded * decode_gain[None, :]).astype(jnp.bfloat16)
    projected, dec_squares = head_terms(
        normed,
        (decode_query, decode_key, decode_value),
        jnp.sum(embedded * embedded, axis=1),
        row_groups,
    )
    projected = projected * row_scale(dec_squares)[:, None]
    positions = (cache_lengths[:, None] + step_ids[None, :]).reshape(own_tokens, 1)
    queries = rotate(
        projected[:, :query_cols].reshape(own_tokens, local_heads, HEAD_DIM), positions
    ).astype(jnp.bfloat16)
    keys_new = rotate(
        projected[:, query_cols : query_cols + kv_cols].reshape(own_tokens, local_kv, HEAD_DIM),
        positions,
    ).astype(jnp.bfloat16)
    values_new = projected[:, query_cols + kv_cols :].astype(jnp.bfloat16)
    queries = queries.reshape(own_passages, step_count, local_kv, group_size, HEAD_DIM)
    keys_new = keys_new.reshape(own_passages, step_count, local_kv, HEAD_DIM)
    values_new = values_new.reshape(own_passages, step_count, local_kv, HEAD_DIM)
    capacity = cache_keys.shape[1]
    keys_old = cache_keys.reshape(own_passages, capacity, local_kv, HEAD_DIM)
    values_old = cache_values.reshape(own_passages, capacity, local_kv, HEAD_DIM)
    new_scores = (
        jnp.einsum("rskgd,rtkd->rskgt", queries, keys_new, preferred_element_type=jnp.float32)
        * score_scale
    )
    causal = step_ids[None, :] <= step_ids[:, None]
    new_scores = jnp.where(causal[None, :, None, None, :], new_scores, -jnp.inf)
    old_scores = (
        jnp.einsum("rskgd,rckd->rskgc", queries, keys_old, preferred_element_type=jnp.float32)
        * score_scale
    )
    slot_ids = jnp.arange(capacity, dtype=jnp.int32)
    live_mask = slot_ids[None, :] < cache_lengths[:, None]
    old_scores = jnp.where(live_mask[:, None, None, None, :], old_scores, -jnp.inf)
    highest = jnp.maximum(jnp.max(old_scores, axis=-1), jnp.max(new_scores, axis=-1))
    old_exp = jnp.exp(old_scores - highest[..., None])
    new_exp = jnp.exp(new_scores - highest[..., None])
    summed = jnp.sum(old_exp, axis=-1) + jnp.sum(new_exp, axis=-1)
    old_weights = (old_exp / summed[..., None]).astype(jnp.bfloat16)
    new_weights = (new_exp / summed[..., None]).astype(jnp.bfloat16)
    attended = jnp.einsum(
        "rskgc,rckd->rskgd", old_weights, values_old, preferred_element_type=jnp.float32
    )
    attended = attended + jnp.einsum(
        "rskgt,rtkd->rskgd", new_weights, values_new, preferred_element_type=jnp.float32
    )
    attended = attended.reshape(own_tokens, query_cols).astype(jnp.bfloat16)
    partial_value = head_mix(attended, decode_out)
    summary = (embedded + width_total(partial_value)).astype(jnp.bfloat16)
    summary_wide = summary.astype(jnp.float32)
    normed_red = (summary_wide * reduce_gain[None, :]).astype(jnp.bfloat16)
    passage_index = jnp.arange(passage_count, dtype=jnp.int32)
    earlier = jnp.sum(
        (
            (doc_ids[None, :] == doc_ids[:, None])
            & (passage_index[None, :] < passage_index[:, None])
        ).astype(jnp.int32),
        axis=1,
    )
    doc_positions = (earlier[:, None] * step_count + step_ids[None, :]).reshape(token_count, 1)
    doc_tokens = (doc_ids[:, None] + jnp.zeros_like(step_ids)[None, :]).reshape(token_count)
    own_positions = lax.dynamic_slice_in_dim(doc_positions, row_first, own_tokens, 0)
    projected, red_squares = head_terms(
        normed_red,
        (reduce_query, reduce_key, reduce_value),
        jnp.sum(summary_wide * summary_wide, axis=1),
        row_groups,
    )
    projected = projected * row_scale(red_squares)[:, None]
    queries_red = rotate(
        projected[:, :query_cols].reshape(own_tokens, local_heads, HEAD_DIM), own_positions
    ).astype(jnp.bfloat16)
    keys_own = (
        rotate(
            projected[:, query_cols : query_cols + kv_cols].reshape(own_tokens, local_kv, HEAD_DIM),
            own_positions,
        )
        .astype(jnp.bfloat16)
        .reshape(own_tokens, kv_cols)
    )
    values_own = projected[:, query_cols + kv_cols :].astype(jnp.bfloat16)
    kv_red = lax.all_gather(
        jnp.concatenate([keys_own, values_own], axis=1), "rows", axis=0, tiled=True
    )
    keys_red, values_red = (kv_red[:, :kv_cols], kv_red[:, kv_cols:])
    queries_red = queries_red.reshape(own_tokens, local_kv, group_size, HEAD_DIM)
    keys_red = keys_red.reshape(token_count, local_kv, HEAD_DIM)
    values_red = values_red.reshape(token_count, local_kv, HEAD_DIM)
    token_index = jnp.arange(token_count, dtype=jnp.int32)
    own_index = row_first + jnp.arange(own_tokens, dtype=jnp.int32)
    own_docs = lax.dynamic_slice_in_dim(doc_tokens, row_first, own_tokens, 0)
    allowed = (own_docs[:, None] == doc_tokens[None, :]) & (
        token_index[None, :] <= own_index[:, None]
    )
    red_scores = (
        jnp.einsum("tkgd,ukd->tkgu", queries_red, keys_red, preferred_element_type=jnp.float32)
        * score_scale
    )
    red_scores = jnp.where(allowed[:, None, None, :], red_scores, -jnp.inf)
    red_high = jnp.max(red_scores, axis=-1)
    red_exp = jnp.exp(red_scores - red_high[..., None])
    red_weights = (red_exp / jnp.sum(red_exp, axis=-1)[..., None]).astype(jnp.bfloat16)
    red_out = jnp.einsum(
        "tkgu,ukd->tkgd", red_weights, values_red, preferred_element_type=jnp.float32
    )
    red_out = red_out.reshape(own_tokens, query_cols).astype(jnp.bfloat16)
    return (summary_wide + width_total(head_mix(red_out, reduce_out))).astype(jnp.bfloat16)


def solution(mesh):
    return jax.shard_map(
        per_device,
        mesh=mesh,
        in_specs=(
            P(),
            P("rows"),
            P(),
            P("tensor", "rows"),
            P("rows", None, "tensor"),
            P("rows", None, "tensor"),
            P("rows"),
            P("rows", "tensor"),
            P("rows", "tensor"),
            P("rows", "tensor"),
            P("tensor", "rows"),
            P("rows"),
            P("rows", "tensor"),
            P("rows", "tensor"),
            P("rows", "tensor"),
            P("tensor", "rows"),
        ),
        out_specs=P(None, "rows"),
        check_vma=False,
    )
```

profile of v0, /device:TPU:8, one launch (start us, length us, event | category | flops | bytes accessed | tf_op | source)
XLA Modules:
  0.0 927.0 jit_solution(14804765056638584329)
XLA Ops:
  6.5 0.9 subtract_clamp_fusion
  7.4 0.1 copy.34
  7.5 0.1 min.18
  7.7 0.1 min.16
  7.8 0.7 compare_and_fusion.1
  8.5 0.2 copy.33
  8.7 0.1 and.30
  8.8 6.2 gather_fusion
  15.0 1.1 select_select_fusion
  16.3 69.0 %all-reduce.6.cloned.1.call-done = bf16[1024,256]{1,0:T(8,128)(2,1)} async-done(((bf16[1024,256]{1,0:T(8,128)(2,1)}), bf16[1024,256]{1,0:T(8,128)(2,1)}) %all-reduce.6.cloned.1.call-update) | async-done | bytes 524304 | tf_op jit(solution)/shard_map/psum | solution.py:30
  85.3 2.0 fusion.41
  87.4 0.3 fusion.37
  87.7 0.3 fusion.39
  88.0 2.8 pad_maximum_fusion.2
  90.8 5.9 copy.36
  96.7 5.6 reshape.597
  102.3 0.2 fusion.22
  102.5 5.2 pad_maximum_fusion
  107.7 6.8 reshape.599
  114.6 0.6 copy-done.12
  115.2 0.2 convert_reduce_fusion
  115.5 0.1 add.142
  115.8 0.5 iota_compare_fusion.3
  116.4 0.2 multiply_cosine_fusion
  116.7 0.3 copy-done.17
  116.9 209.4 %reduce-scatter.7.cloned.1.call-done = f32[1,8,5124]{2,1,0:T(8,128)} async-done(((f32[32,8,5124]{2,1,0:T(8,128)}), f32[1,8,5124]{2,1,0:T(8,128)}) %reduce-scatter.7.cloned.1.call-update) | async-done | bytes 163984
  326.3 1.0 reshape.600
  327.4 0.5 fusion.75
  327.9 0.9 broadcast_multiply_fusion.1
  328.9 0.8 fusion.65
  329.9 1.1 fusion.81
  331.0 0.5 fusion.82
  331.6 0.3 fusion.8
  331.9 0.2 fusion.49
  332.2 0.6 fusion.15
  332.7 0.6 copy.58
  333.5 76.0 %all-gather.3.cloned.1.call-done = bf16[1024,1024]{1,0:T(8,128)(2,1)} async-done(((bf16[32,1024]{1,0:T(8,128)(2,1)}), bf16[1024,1024]{1,0:T(8,128)(2,1)}) %all-gather.3.cloned.1.call-update) | async-done | bytes 2097168 | tf_op jit(solution)/shard_map/all_gather | solution.py:53
  409.5 3.3 fusion.84
  412.8 0.2 reduce-scatter.9.cloned.1.call-start
  413.0 66.1 %all-reduce.8.cloned.1.call-done = f32[1024,256]{1,0:T(8,128)} async-done(((f32[1024,256]{1,0:T(8,128)}), f32[1024,256]{1,0:T(8,128)}) %all-reduce.8.cloned.1.call-update) | async-done | bytes 1048592 | tf_op jit(solution)/shard_map/psum | solution.py:30
  479.1 1.4 fusion.25
  480.6 0.8 fusion.35
  481.4 0.1 copy-done.8
  481.5 0.3 fusion.31
  481.8 0.3 fusion.33
  482.1 2.9 pad_maximum_fusion.3
  485.1 5.9 copy.37
  491.0 5.6 reshape.607
  496.6 5.2 pad_maximum_fusion.1
  501.8 6.8 reshape.609
  508.6 0.6 copy-done.13
  509.3 0.1 reshape.613
  509.6 211.0 %reduce-scatter.9.cloned.1.call-done = f32[1,8,5124]{2,1,0:T(8,128)} async-done(((f32[32,8,5124]{2,1,0:T(8,128)}), f32[1,8,5124]{2,1,0:T(8,128)}) %reduce-scatter.9.cloned.1.call-update) | async-done | bytes 163984
  720.6 1.0 reshape.610
  721.9 0.1 fusion.71
  722.1 47.8 %all_gather.10 = bf16[1024,256]{1,0:T(8,128)(2,1)S(1)} all-gather(bf16[32,256]{1,0:T(8,128)(2,1)S(1)} %pad_maximum_fusion.5), channel_id=1, replica_groups=mesh['rows'=32,'tensor'=8] {'rows'}, dimensions={0}, use_global_device_ids=true | all-gather | bytes 540672 | tf_op jit(solution)/shard_map/all_gather | solution.py:180
  770.0 0.4 fusion.83
  770.4 0.3 fusion.27
  770.8 0.4 fusion.18
  771.2 0.6 copy.57
  771.9 76.5 %all-gather.5.cloned.1.call-done = bf16[1024,1024]{1,0:T(8,128)(2,1)} async-done(((bf16[32,1024]{1,0:T(8,128)(2,1)}), bf16[1024,1024]{1,0:T(8,128)(2,1)}) %all-gather.5.cloned.1.call-update) | async-done | bytes 2097168 | tf_op jit(solution)/shard_map/all_gather | solution.py:53
  848.4 3.4 fusion.85
  851.8 66.3 %all-reduce.10.cloned.1.call-done = f32[1024,256]{1,0:T(8,128)} async-done(((f32[1024,256]{1,0:T(8,128)}), f32[1024,256]{1,0:T(8,128)}) %all-reduce.10.cloned.1.call-update) | async-done | bytes 1048592 | tf_op jit(solution)/shard_map/psum | solution.py:30
  918.1 2.1 fusion.26
  (93 shorter events, 2.0 us)
Async XLA Ops:
  6.5 323.3 %copy-start = (bf16[8,1280,128]{2,1,0:T(8,128)(2,1)S(1)}, bf16[8,1280,128]{2,1,0:T(8,128)(2,1)}, u32[]{:S(2)}) copy-start(bf16[8,1280,128]{2,1,0:T(8,128)(2,1)} %param.20) | copy-start | bytes 7864324
  6.5 78.8 %copy-start.10 = (f32[256]{0:T(256)S(1)}, f32[256]{0:T(256)}, u32[]{:S(2)}) copy-start(f32[256]{0:T(256)} %param.22) | copy-start | bytes 3076
  6.5 78.8 %all-reduce.6.cloned.1.call-start = ((), (), s32[]{:S(2)}) async-start(), calls=%async_computation.2 | async-start | bytes 1048576 | tf_op jit(solution)/shard_map/psum | solution.py:30
  16.2 71.1 %copy-start.6 = (bf16[256,128]{1,0:T(8,128)(2,1)S(1)}, bf16[256,128]{1,0:T(8,128)(2,1)}, u32[]{:S(2)}) copy-start(bf16[256,128]{1,0:T(8,128)(2,1)} %param.25) | copy-start | bytes 196612
  16.2 71.5 %copy-start.7 = (bf16[256,128]{1,0:T(8,128)(2,1)S(1)}, bf16[256,128]{1,0:T(8,128)(2,1)}, u32[]{:S(2)}) copy-start(bf16[256,128]{1,0:T(8,128)(2,1)} %param.24) | copy-start | bytes 196612
  16.2 310.1 %reduce-scatter.7.cloned.1.call-start = ((), (), s32[]{:S(2)}) async-start(), calls=%async_computation.7 | async-start | bytes 5541888
  85.3 2.0 copy-start.2
  114.5 0.7 copy-start.12
  114.5 1.1 copy-start.19
  114.5 295.0 %all-gather.3.cloned.1.call-start = ((), (), s32[]{:S(2)}) async-start(), calls=%async_computation.3 | async-start | bytes 2162688 | tf_op jit(solution)/shard_map/all_gather | solution.py:53
  115.8 0.9 copy-start.16
  115.8 0.9 copy-start.14
  116.4 0.6 copy-start.17
  327.9 3.1 copy-start.22
  327.9 4.2 copy-start.20
  331.9 77.6 %copy-start.21 = (bf16[1024,256]{1,0:T(8,128)(2,1)S(1)}, bf16[1024,256]{1,0:T(8,128)(2,1)}, u32[]{:S(2)}) copy-start(bf16[1024,256]{1,0:T(8,128)(2,1)} %param.26) | copy-start | bytes 1572868
  333.4 147.1 %copy-start.5 = (bf16[256,1024]{1,0:T(8,128)(2,1)S(1)}, bf16[256,1024]{1,0:T(8,128)(2,1)}, u32[]{:S(2)}) copy-start(bf16[256,1024]{1,0:T(8,128)(2,1)} %param.28) | copy-start | bytes 1572868
  333.4 147.1 %copy-start.11 = (f32[256]{0:T(256)S(1)}, f32[256]{0:T(256)}, u32[]{:S(2)}) copy-start(f32[256]{0:T(256)} %param.27) | copy-start | bytes 3076
  333.4 145.7 %all-reduce.8.cloned.1.call-start = ((), (), s32[]{:S(2)}) async-start(), calls=%async_computation.4 | async-start | bytes 2097152 | tf_op jit(solution)/shard_map/psum | solution.py:30
  412.8 307.8 %reduce-scatter.9.cloned.1.call-start = ((), (), s32[]{:S(2)}) async-start(), calls=%async_computation.8 | async-start | bytes 5541888
  480.5 1.3 copy-start.3
  480.6 0.9 copy-start.8
  480.6 1.2 copy-start.9
  508.6 0.7 copy-start.13
  508.6 213.3 %copy-start.15 = (f32[64]{0:T(128)S(1)}, f32[64]{0:T(128)}, u32[]{:S(2)}) copy-start(f32[64]{0:T(128)} %copy-done.14) | copy-start | bytes 772
  508.6 213.3 %copy-start.18 = (f32[32]{0:T(128)S(1)}, f32[32]{0:T(128)}, u32[]{:S(2)}) copy-start(f32[32]{0:T(128)} %copy-done.17) | copy-start | bytes 388
  508.6 339.8 %all-gather.5.cloned.1.call-start = ((), (), s32[]{:S(2)}) async-start(), calls=%async_computation.5 | async-start | bytes 2162688 | tf_op jit(solution)/shard_map/all_gather | solution.py:53
  771.1 146.9 %copy-start.4 = (bf16[1024,256]{1,0:T(8,128)(2,1)S(1)}, bf16[1024,256]{1,0:T(8,128)(2,1)}, u32[]{:S(2)}) copy-start(bf16[1024,256]{1,0:T(8,128)(2,1)} %copy-done.3) | copy-start | bytes 1572868
  771.8 148.4 %copy-start.1 = (bf16[8,1280,128]{2,1,0:T(8,128)(2,1)S(1)}, bf16[8,1280,128]{2,1,0:T(8,128)(2,1)}, u32[]{:S(2)}) copy-start(bf16[8,1280,128]{2,1,0:T(8,128)(2,1)} %param.20) | copy-start | bytes 7864324
  771.8 146.2 %all-reduce.10.cloned.1.call-start = ((), (), s32[]{:S(2)}) async-start(), calls=%async_computation.6 | async-start | bytes 2097152 | tf_op jit(solution)/shard_map/psum | solution.py:30
Sparse Core Ops, SparseCore 0:
  16.3 68.9 all-reduce.5
  114.6 211.6 reduce-scatter.6
  333.5 75.9 all-gather.2
  412.9 66.1 all-reduce.7
  508.7 211.8 reduce-scatter.8
  771.9 76.3 all-gather.4
  851.9 66.1 all-reduce.9
where the time goes:
time: 928 us; the launch traced here: 927 us
  waiting for transfers between devices  774 us (83%)
  local copies, waits for them, and re-layouts  49.3 us (5%)
  blocking collectives  47.8 us (5%)
  other arithmetic  27.3 us (3%)
  between operations  14 us (2%)
  matrix products  13.9 us (1%)
    unnamed x9, waiting for transfers between devices  420 us
    psum x3, waiting for transfers between devices, width_total(): return lax.psum(partial_value, 'tensor')  201 us
    all_gather x2, waiting for transfers between devices, head_mix(): lax.all_gather(attended, 'rows', axis=0, tiled=True)  153 us
    all_gather x1, blocking collectives, per_device(): lax.all_gather(jnp.concatenate([keys_own, values_own], axis=1), 'rows', a...  47.8 us
  transfers between devices with their start and end apart: 7, of which 7 were waited for; matrix products, arithmetic and copies ran while one was open for 0% of the time, Pallas kernels for 0%

commit v1 on v0

--- a/solution.py
+++ b/solution.py
@@ -1,12 +1,22 @@
+import functools
 import jax
 import jax.numpy as jnp
 from jax import lax
 from jax.sharding import PartitionSpec as P
+from jax.lax import all_gather
 
 D = 8192
 HEAD_DIM = 128
 EPSILON = 1e-05
 ROPE_BASE = 500000.0
+
+
+def assign_sample_by_axis(tile_in, a_name):
+    ready = jnp.sum(all_gather(tile_in, axis_name=a_name), 0)
+    return ready
+
+
+turn_series = functools.partial(assign_sample_by_axis, a_name="tensor")
 
 
 def rotate(vectors, positions):
@@ -27,7 +37,7 @@
 
 
 def width_total(partial_value):
-    return lax.psum(partial_value, "tensor")
+    return turn_series(partial_value)
 
 
 def row_scale(summed):

time: 928 us -> 880 us (0.948)
  waiting for transfers between devices: 774 us -> 714 us
  other arithmetic: 27.3 us -> 38.6 us
    psum x3 -> x0, waiting for transfers between devices: 201 us -> none  [width_total(): return lax.psum(partial_value, 'tensor')]
    all_gather x0 -> x3, waiting for transfers between devices: none -> 139 us  [assign_sample_by_axis(): ready = jnp.sum(all_gather(tile_in, axis_name=a_name), 0)]
    reduce_sum x0 -> x3, other arithmetic: none -> 12.5 us  [assign_sample_by_axis(): ready = jnp.sum(all_gather(tile_in, axis_name=a_name), 0)]
where the time goes in v1:
time: 880 us; the launch traced here: 877 us
  waiting for transfers between devices  714 us (81%)
  local copies, waits for them, and re-layouts  49.3 us (6%)
  blocking collectives  47.7 us (5%)
  other arithmetic  38.6 us (4%)
  between operations  14 us (2%)
  matrix products  13.8 us (2%)
    unnamed x9, waiting for transfers between devices  422 us
    all_gather x2, waiting for transfers between devices, head_mix(): lax.all_gather(attended, 'rows', axis=0, tiled=True)  153 us
    all_gather x3, waiting for transfers between devices, assign_sample_by_axis(): ready = jnp.sum(all_gather(tile_in, axis_name=a_name), 0)  139 us
    all_gather x1, blocking collectives, per_device(): lax.all_gather(jnp.concatenate([keys_own, values_own], axis=1), 'rows', a...  47.7 us
  transfers between devices with their start and end apart: 7, of which 7 were waited for; matrix products, arithmetic and copies ran while one was open for 0% of the time, Pallas kernels for 0%

profile of v1, /device:TPU:8, one launch (start us, length us, event | category | flops | bytes accessed | tf_op | source)
XLA Modules:
  0.0 877.4 jit_solution(1633372569032818856)
XLA Ops:
  6.5 0.8 subtract_clamp_fusion
  7.4 0.1 copy.34
  7.5 0.1 min.18
  7.8 0.7 compare_and_fusion.1
  8.5 0.2 copy.33
  8.7 0.1 and.30
  8.8 6.2 gather_fusion
  15.0 1.1 fusion.31
  16.2 37.6 %all-gather.8.cloned.1.call-done = bf16[8,1024,256]{2,1,0:T(8,128)(2,1)} async-done(((bf16[1,1024,256]{2,1,0:T(8,128)(2,1)}), bf16[8,1024,256]{2,1,0:T(8,128)(2,1)}) %all-gather.8.cloned.1.call-update) | async-done | bytes 4194320 | tf_op jit(solution)/shard_map/all_gather | solution.py:15
  53.8 3.0 reduce_sum.84
  56.9 0.2 fusion.22
  57.1 1.8 fusion.42
  58.9 0.3 fusion.38
  59.3 0.3 fusion.40
  59.6 2.8 pad_maximum_fusion.2
  62.4 5.9 copy.36
  68.3 5.6 reshape.642
  73.9 5.2 pad_maximum_fusion
  79.1 6.8 reshape.644
  86.0 0.6 copy-done.11
  86.6 0.2 convert_reduce_fusion
  87.2 0.5 iota_compare_fusion.3
  87.8 0.2 multiply_cosine_fusion
  88.1 0.3 copy-done.16
  88.3 210.3 %reduce-scatter.7.cloned.1.call-done = f32[1,8,5124]{2,1,0:T(8,128)} async-done(((f32[32,8,5124]{2,1,0:T(8,128)}), f32[1,8,5124]{2,1,0:T(8,128)}) %reduce-scatter.7.cloned.1.call-update) | async-done | bytes 163984
  298.6 1.0 reshape.645
  299.6 0.5 fusion.76
  300.2 0.9 broadcast_multiply_fusion.1
  301.2 0.8 fusion.66
  302.1 1.1 fusion.82
  303.3 0.5 fusion.83
  303.8 0.3 fusion.8
  304.2 0.2 fusion.50
  304.4 0.6 fusion.15
  305.0 0.6 copy.58
  305.7 76.0 %all-gather.10.cloned.1.call-done = bf16[1024,1024]{1,0:T(8,128)(2,1)} async-done(((bf16[32,1024]{1,0:T(8,128)(2,1)}), bf16[1024,1024]{1,0:T(8,128)(2,1)}) %all-gather.10.cloned.1.call-update) | async-done | bytes 2097168 | tf_op jit(solution)/shard_map/all_gather | solution.py:63
  381.8 3.4 fusion.85
  385.2 0.2 reduce-scatter.9.cloned.1.call-start
  385.4 50.6 %all-gather.14.cloned.1.call-done = f32[8192,256]{1,0:T(8,128)} async-done(((f32[1024,256]{1,0:T(8,128)}), f32[8192,256]{1,0:T(8,128)}) %all-gather.14.cloned.1.call-update) | async-done | bytes 8388624 | tf_op jit(solution)/shard_map/all_gather | solution.py:15
  436.0 4.1 reduce_sum.88
  440.1 0.2 fusion.25
  440.4 0.8 fusion.36
  441.1 0.1 copy-done.7
  441.3 0.3 fusion.32
  441.6 0.3 fusion.34
  441.9 2.9 pad_maximum_fusion.3
  444.8 5.9 copy.37
  450.7 5.6 reshape.652
  456.4 5.2 pad_maximum_fusion.1
  461.6 6.8 reshape.654
  468.4 0.6 copy-done.12
  469.4 211.8 %reduce-scatter.9.cloned.1.call-done = f32[1,8,5124]{2,1,0:T(8,128)} async-done(((f32[32,8,5124]{2,1,0:T(8,128)}), f32[1,8,5124]{2,1,0:T(8,128)}) %reduce-scatter.9.cloned.1.call-update) | async-done | bytes 163984
  681.3 1.0 reshape.655
  682.5 0.1 fusion.72
  682.7 47.7 %all_gather.29 = bf16[1024,256]{1,0:T(8,128)(2,1)S(1)} all-gather(bf16[32,256]{1,0:T(8,128)(2,1)S(1)} %pad_maximum_fusion.5), channel_id=1, replica_groups=mesh['rows'=32,'tensor'=8] {'rows'}, dimensions={0}, use_global_device_ids=true | all-gather | bytes 540672 | tf_op jit(solution)/shard_map/all_gather | solution.py:190
  730.6 0.4 fusion.84
  731.0 0.3 fusion.27
  731.3 0.4 fusion.18
  731.7 0.6 copy.57
  732.4 76.5 %all-gather.12.cloned.1.call-done = bf16[1024,1024]{1,0:T(8,128)(2,1)} async-done(((bf16[32,1024]{1,0:T(8,128)(2,1)}), bf16[1024,1024]{1,0:T(8,128)(2,1)}) %all-gather.12.cloned.1.call-update) | async-done | bytes 2097168 | tf_op jit(solution)/shard_map/all_gather | solution.py:63
  808.9 3.4 fusion.86
  812.3 50.8 %all-gather.16.cloned.1.call-done = f32[8192,256]{1,0:T(8,128)} async-done(((f32[1024,256]{1,0:T(8,128)}), f32[8192,256]{1,0:T(8,128)}) %all-gather.16.cloned.1.call-update) | async-done | bytes 8388624 | tf_op jit(solution)/shard_map/all_gather | solution.py:15
  863.1 5.3 reduce_sum.92
  868.4 2.1 fusion.26
  (96 shorter events, 2.4 us)
Async XLA Ops:
  6.5 295.6 %copy-start = (bf16[8,1280,128]{2,1,0:T(8,128)(2,1)S(1)}, bf16[8,1280,128]{2,1,0:T(8,128)(2,1)}, u32[]{:S(2)}) copy-start(bf16[8,1280,128]{2,1,0:T(8,128)(2,1)} %param.20) | copy-start | bytes 7864324
  6.5 47.3 %all-gather.8.cloned.1.call-start = ((), (), s32[]{:S(2)}) async-start(), calls=%async_computation.2 | async-start | bytes 4718592 | tf_op jit(solution)/shard_map/all_gather | solution.py:15
  15.0 42.0 %copy-start.9 = (f32[256]{0:T(256)S(1)}, f32[256]{0:T(256)}, u32[]{:S(2)}) copy-start(f32[256]{0:T(256)} %param.22) | copy-start | bytes 3076
  16.2 282.4 %reduce-scatter.7.cloned.1.call-start = ((), (), s32[]{:S(2)}) async-start(), calls=%async_computation.7 | async-start | bytes 5541888
  57.1 1.9 copy-start.5
  57.1 2.2 copy-start.6
  85.9 0.7 copy-start.11
  85.9 1.1 copy-start.18
  85.9 295.9 %all-gather.10.cloned.1.call-start = ((), (), s32[]{:S(2)}) async-start(), calls=%async_computation.3 | async-start | bytes 2162688 | tf_op jit(solution)/shard_map/all_gather | solution.py:63
  87.1 0.9 copy-start.15
  87.2 0.9 copy-start.13
  87.8 0.6 copy-start.16
  300.2 3.1 copy-start.22
  300.2 4.2 copy-start.19
  304.2 77.6 %copy-start.20 = (bf16[1024,256]{1,0:T(8,128)(2,1)S(1)}, bf16[1024,256]{1,0:T(8,128)(2,1)}, u32[]{:S(2)}) copy-start(bf16[1024,256]{1,0:T(8,128)(2,1)} %param.26) | copy-start | bytes 1572868
  305.7 130.3 %all-gather.14.cloned.1.call-start = ((), (), s32[]{:S(2)}) async-start(), calls=%async_computation.5 | async-start | bytes 9437184 | tf_op jit(solution)/shard_map/all_gather | solution.py:15
  385.2 296.1 %reduce-scatter.9.cloned.1.call-start = ((), (), s32[]{:S(2)}) async-start(), calls=%async_computation.8 | async-start | bytes 5541888
  436.0 4.4 copy-start.4
  436.0 4.4 copy-start.10
  440.3 1.3 copy-start.2
  440.3 0.9 copy-start.7
  440.3 1.2 copy-start.8
  468.3 0.7 copy-start.12
  468.3 214.2 %copy-start.14 = (f32[64]{0:T(128)S(1)}, f32[64]{0:T(128)}, u32[]{:S(2)}) copy-start(f32[64]{0:T(128)} %copy-done.13) | copy-start | bytes 772
  468.3 214.2 %copy-start.17 = (f32[32]{0:T(128)S(1)}, f32[32]{0:T(128)}, u32[]{:S(2)}) copy-start(f32[32]{0:T(128)} %copy-done.16) | copy-start | bytes 388
  468.4 340.6 %all-gather.12.cloned.1.call-start = ((), (), s32[]{:S(2)}) async-start(), calls=%async_computation.4 | async-start | bytes 2162688 | tf_op jit(solution)/shard_map/all_gather | solution.py:63
  730.4 78.5 %copy-start.21 = (bf16[1024,256]{1,0:T(8,128)(2,1)S(1)}, bf16[1024,256]{1,0:T(8,128)(2,1)}, u32[]{:S(2)}) copy-start(bf16[1024,256]{1,0:T(8,128)(2,1)} %param.31) | copy-start | bytes 1572868
  732.4 130.7 %all-gather.16.cloned.1.call-start = ((), (), s32[]{:S(2)}) async-start(), calls=%async_computation.6 | async-start | bytes 9437184 | tf_op jit(solution)/shard_map/all_gather | solution.py:15
  863.1 7.4 copy-start.1
  863.1 5.3 copy-start.3
Sparse Core Ops, SparseCore 0:
  16.3 37.4 all-gather.7
  86.0 212.5 reduce-scatter.6
  305.8 75.9 all-gather.9
  385.3 50.6 all-gather.13
  468.5 212.7 reduce-scatter.8
  732.5 76.3 all-gather.11
  812.4 50.6 all-gather.15
